TPU v7x, 32 devices: a whole 2x2x4 slice. The times are simulated.
32 devices in a mesh: blk: 8 (over z, y), grp: 4 (over x, core).
Axes of the slice: x: 2, y: 2, z: 4, core: 2. Of those that a mesh axis runs over, the one named last changes fastest.
Arguments:
- hidden: bfloat16 [65536, 384], P(('blk', 'grp')), may hold values from -6 to 6
- cotangent: bfloat16 [65536, 384], P(('blk', 'grp')), may hold values from -6 to 6
- token_ids: int32 [65536], P(('blk', 'grp')), may hold values from 0 to 32127, as said below
- w_in: bfloat16 [8, 4, 384, 1536], P('blk', 'grp'), may hold values from -6 to 6
- w_out: bfloat16 [1536, 384], replicated, may hold values from -0.15625 to 0.15625
- tracker: bfloat16 [8, 4, 384, 1536], P('blk', 'grp'), may hold values from -6 to 6
- grad_old: bfloat16 [8, 4, 384, 1536], P('blk', 'grp'), may hold values from -6 to 6
- cheb_num: int32 [4], replicated, may hold values from 10 to 16
- cheb_den: int32 [4], replicated, may hold values from 9 to 11
Outputs:
- new_params: bfloat16 [8, 4, 384, 1536], P('blk', 'grp')
- new_tracker: bfloat16 [8, 4, 384, 1536], P('blk', 'grp')
Inputs may be any that keep to these rules, and one draw needn't show every extreme that they name: `token_ids`: each aligned run of 512 rows is one sequence: ids from 1 to 32127 up to its length, 0 after it; every length is 128 or more.
All inputs are finite; a program needn't handle non-finite values.
Results may differ from a plain program's by a relative error of at most 0.013.
Values may be sent and summed in bfloat16 or wider, within the bound.
A program may use at most 128 MiB of HBM per device.

v0:
```python
import math

import jax
import jax.numpy as jnp
from jax import lax
from jax.sharding import PartitionSpec as P

ROUNDS = 4


epsilon = 1e-06
step_size = 0.25
tanh_scale = math.sqrt(2.0 / math.pi)


def padded(cells, sides, width):
    for axis, dim in sides:
        count = lax.axis_size(axis)
        head = lax.slice_in_dim(cells, 0, width, axis=dim)
        tail = lax.slice_in_dim(cells, cells.shape[dim] - width, cells.shape[dim], axis=dim)
        cells = jnp.concatenate(
            [
                lax.ppermute(tail, axis, [(i, (i + 1) % count) for i in range(count)]),
                cells,
                lax.ppermute(head, axis, [((i + 1) % count, i) for i in range(count)]),
            ],
            axis=dim,
        )
    return cells


def passed_along(value, axis, by):
    devices = lax.axis_size(axis)
    return lax.ppermute(value, axis, [(i, (i + by) % devices) for i in range(devices)])


def gelu_slope(values):
    cubic = values * values * values
    bent_tanh = jnp.tanh(tanh_scale * (values + 0.044715 * cubic))
    return 0.5 * (1.0 + bent_tanh) + 0.5 * values * (1.0 - bent_tanh * bent_tanh) * tanh_scale * (
        1.0 + 3.0 * 0.044715 * values * values
    )


def cycle_mean(beside_all):
    return ((beside_all[0] + beside_all[1] + beside_all[2]) / 3.0)[None]


def local_grad(hidden, cotangent, token_ids, params, w_out):
    widened = hidden.astype(jnp.float32)
    mean_square = jnp.mean(widened * widened, axis=-1, keepdims=True)
    normed = (widened * lax.rsqrt(mean_square + epsilon)).astype(jnp.bfloat16)
    inv_root = params.shape[0] ** (-0.5)
    pre_act = jnp.dot(normed, params, preferred_element_type=jnp.float32) * inv_root
    masked = jnp.where((token_ids != 0)[:, None], cotangent, jnp.zeros_like(cotangent))
    back_flow = lax.dot_general(
        masked, w_out, (((1,), (1,)), ((), ())), preferred_element_type=jnp.float32
    )
    slope_bf = (back_flow * gelu_slope(pre_act)).astype(jnp.bfloat16)
    return (
        lax.dot_general(
            normed, slope_bf, (((0,), (0,)), ((), ())), preferred_element_type=jnp.float32
        )
        * inv_root
    )


def shards(hidden, cotangent, token_ids, w_in, w_out, tracker, grad_old, cheb_num, cheb_den):
    beside_all = padded(w_in, (("blk", 0),), 1).astype(jnp.float32)
    cycle_mixed = cycle_mean(beside_all)
    groups = lax.axis_size("grp")
    group_sum = lax.psum(cycle_mixed.astype(jnp.bfloat16), "grp").astype(jnp.float32)
    group_avg = group_sum / groups
    new_params = (group_avg - step_size * tracker.astype(jnp.float32)).astype(jnp.bfloat16)
    weights = cheb_num.astype(jnp.float32) / cheb_den.astype(jnp.float32)
    start_iter = tracker.astype(jnp.float32)
    coeffs = jnp.zeros((2 * ROUNDS + 1,), jnp.float32).at[ROUNDS].set(1.0)
    older_coef = coeffs
    current_coef = coeffs
    for turn_idx in range(ROUNDS):
        mixed_coef = (jnp.roll(current_coef, 1) + current_coef + jnp.roll(current_coef, -1)) / 3.0
        next_coef = weights[turn_idx] * mixed_coef + (1.0 - weights[turn_idx]) * older_coef
        older_coef, current_coef = (current_coef, next_coef)
    consensus = current_coef[ROUNDS] * start_iter
    for hop_len in range(1, ROUNDS + 1):
        for direction in (1, -1):
            shifted = passed_along(tracker, "blk", direction * hop_len)
            consensus = consensus + current_coef[ROUNDS + direction * hop_len] * shifted.astype(
                jnp.float32
            )
    grad_new = local_grad(hidden, cotangent, token_ids, new_params[0, 0], w_out)[None, None]
    new_tracker = (consensus + grad_new - grad_old.astype(jnp.float32)).astype(jnp.bfloat16)
    return (new_params, new_tracker)


def solution(mesh):
    placed = (
        P(("blk", "grp"), None),
        P(("blk", "grp"), None),
        P(("blk", "grp")),
        P("blk", "grp", None, None),
        P(),
        P("blk", "grp", None, None),
        P("blk", "grp", None, None),
        P(),
        P(),
    )
    return jax.shard_map(
        shards,
        mesh=mesh,
        in_specs=placed,
        out_specs=(P("blk", "grp", None, None), P("blk", "grp", None, None)),
        check_vma=False,
    )
```

profile of v0, /device:TPU:13, one launch (start us, length us, event | category | flops | bytes accessed | tf_op | source)
XLA Modules:
  0.0 272.7 jit_solution(17097729729248453271)
XLA Ops:
  7.2 1.3 collective-permute-start
  8.5 0.2 collective-permute-start.1
  8.7 3.2 %collective-permute-start.6 = (bf16[1,1,384,1536]{3,2,1,0:T(8,128)(2,1)}, bf16[1,1,384,1536]{3,2,1,0:T(8,128)(2,1)}, u32[]{:S(2)}, u32[]{:S(2)}) collective-permute-start(bf16[1,1,384,1536]{3,2,1,0:T(8,128)(2,1)} %param.16), channel_id=1, source_target_pairs={{0,12},{4,16},{8,20},{12,24},{16,28},{20,0},{24,4},{28,8},{1,13},{... | collective-permute-start | bytes 3538952 | tf_op jit(solution)/shard_map/ppermute | solution.py:34
  11.9 0.2 collective-permute-start.5
  12.1 1.3 collective-permute-start.4
  13.4 0.7 convert_divide_fusion
  14.0 0.6 fusion.49
  17.1 0.7 multiply_add_fusion.3
  17.8 0.1 fusion.55
  17.9 0.6 fusion.54
  18.5 1.9 multiply_add_fusion.2
  23.0 0.6 fusion.52
  23.6 0.1 fusion.53
  23.6 1.4 multiply_add_fusion.1
  25.0 0.6 fusion.50
  25.6 0.1 fusion.51
  25.7 1.4 multiply_add_fusion
  27.0 57.9 %collective-permute-done = bf16[1,1,384,1536]{3,2,1,0:T(8,128)(2,1)S(1)} collective-permute-done((bf16[1,1,384,1536]{3,2,1,0:T(8,128)(2,1)}, bf16[1,1,384,1536]{3,2,1,0:T(8,128)(2,1)S(1)}, u32[]{:S(2)}, u32[]{:S(2)}) %collective-permute-start) | collective-permute-done | bytes 1179680 | tf_op jit(solution)/shard_map/ppermute | solution.py:23
  84.9 0.1 collective-permute-done.1
  85.0 2.7 %collective-permute-start.2 = (bf16[1,1,384,1536]{3,2,1,0:T(8,128)(2,1)}, bf16[1,1,384,1536]{3,2,1,0:T(8,128)(2,1)}, u32[]{:S(2)}, u32[]{:S(2)}) collective-permute-start(bf16[1,1,384,1536]{3,2,1,0:T(8,128)(2,1)} %param.16), channel_id=1, source_target_pairs={{0,4},{4,8},{8,12},{12,16},{16,20},{20,24},{24,28},{28,0},{1,5},{5... | collective-permute-start | bytes 3538952 | tf_op jit(solution)/shard_map/ppermute | solution.py:34
  87.7 1.8 maximum_convert_fusion
  89.5 1.8 fusion.23
  91.4 0.4 fusion.5
  91.8 0.7 fusion.48
  92.5 16.9 %collective-permute-done.6 = bf16[1,1,384,1536]{3,2,1,0:T(8,128)(2,1)} collective-permute-done((bf16[1,1,384,1536]{3,2,1,0:T(8,128)(2,1)}, bf16[1,1,384,1536]{3,2,1,0:T(8,128)(2,1)}, u32[]{:S(2)}, u32[]{:S(2)}) %collective-permute-start.6) | collective-permute-done | bytes 1179680 | tf_op jit(solution)/shard_map/ppermute | solution.py:34
  109.4 78.7 %collective-permute-done.5 = bf16[1,1,384,1536]{3,2,1,0:T(8,128)(2,1)} collective-permute-done((bf16[1,1,384,1536]{3,2,1,0:T(8,128)(2,1)}, bf16[1,1,384,1536]{3,2,1,0:T(8,128)(2,1)}, u32[]{:S(2)}, u32[]{:S(2)}) %collective-permute-start.5) | collective-permute-done | bytes 1179680 | tf_op jit(solution)/shard_map/ppermute | solution.py:34
  188.1 2.0 fusion.10
  190.2 6.4 %fusion.30 = f32[2048,1536]{1,0:T(8,128)} fusion(bf16[1,1,384,1536]{3,2,1,0:T(8,128)(2,1)S(1)} %fusion.10, bf16[2048,384]{1,0:T(8,128)(2,1)S(1)} %copy-done.1, f32[2048]{0:T(1024)S(1)} %add_rsqrt_fusion), kind=kOutput, calls=%fused_computation.37 | convolution fusion | flops 2418278400 | bytes 15343616 | tf_op jit(solution)/shard_map/dot_general | solution.py:54
  196.6 13.9 %collective-permute-done.2 = bf16[1,1,384,1536]{3,2,1,0:T(8,128)(2,1)} collective-permute-done((bf16[1,1,384,1536]{3,2,1,0:T(8,128)(2,1)}, bf16[1,1,384,1536]{3,2,1,0:T(8,128)(2,1)}, u32[]{:S(2)}, u32[]{:S(2)}) %collective-permute-start.2) | collective-permute-done | bytes 1179680 | tf_op jit(solution)/shard_map/ppermute | solution.py:34
  210.5 25.3 %collective-permute-done.8 = bf16[1,1,384,1536]{3,2,1,0:T(8,128)(2,1)} collective-permute-done((bf16[1,1,384,1536]{3,2,1,0:T(8,128)(2,1)}, bf16[1,1,384,1536]{3,2,1,0:T(8,128)(2,1)}, u32[]{:S(2)}, u32[]{:S(2)}) %collective-permute-start.8) | collective-permute-done | bytes 1179680 | tf_op jit(solution)/shard_map/ppermute | solution.py:34
  235.8 1.9 collective-permute-done.7
  237.7 28.2 %fusion.21 = bf16[1,1,384,1536]{3,2,1,0:T(8,128)(2,1)} fusion(bf16[1,1,384,1536]{3,2,1,0:T(8,128)(2,1)} %param.16, bf16[1,1,384,1536]{3,2,1,0:T(8,128)(2,1)} %collective-permute-done.8, bf16[1,1,384,1536]{3,2,1,0:T(8,128)(2,1)} %param.17, bf16[1,1,384,1536]{3,2,1,0:T(8,128)(2,1)} %collective-permute-done.7, ...), kind=kOutput, calls=%fused_computation.30 | convolution fusion | flops 4915593216 | bytes 28715044 | tf_op jit(solution)/shard_map/dot_general | solution.py:61
  (18 shorter events, 0.1 us)
Async XLA Ops:
  7.2 230.5 %copy-start = (bf16[1536,384]{1,0:T(8,128)(2,1)S(1)}, bf16[1536,384]{1,0:T(8,128)(2,1)}, u32[]{:S(2)}) copy-start(bf16[1536,384]{1,0:T(8,128)(2,1)} %param.15) | copy-start | bytes 3538948
  7.2 180.9 %all-reduce.2.cloned.1.call-start = ((), (), s32[]{:S(2)}) async-start(), calls=%async_computation | async-start | bytes 2359296 | tf_op jit(solution)/shard_map/psum | solution.py:72
  7.2 77.7 %collective-permute-start = (bf16[1,1,384,1536]{3,2,1,0:T(8,128)(2,1)}, bf16[1,1,384,1536]{3,2,1,0:T(8,128)(2,1)S(1)}, u32[]{:S(2)}, u32[]{:S(2)}) collective-permute-start(bf16[1,1,384,1536]{3,2,1,0:T(8,128)(2,1)} %param.14), channel_id=1, source_target_pairs={{0,4},{4,8},{8,12},{12,16},{16,20},{20,24},{24,28},{28,0},{1,5},{5... | collective-permute-start | bytes 3538952 | tf_op jit(solution)/shard_map/ppermute | solution.py:23
  8.5 76.5 %collective-permute-start.1 = (bf16[1,1,384,1536]{3,2,1,0:T(8,128)(2,1)}, bf16[1,1,384,1536]{3,2,1,0:T(8,128)(2,1)S(1)}, u32[]{:S(2)}, u32[]{:S(2)}) collective-permute-start(bf16[1,1,384,1536]{3,2,1,0:T(8,128)(2,1)} %param.14), channel_id=1, source_target_pairs={{4,0},{8,4},{12,8},{16,12},{20,16},{24,20},{28,24},{0,28},{5,1},{9... | collective-permute-start | bytes 3538952 | tf_op jit(solution)/shard_map/ppermute | solution.py:25
  8.7 100.7 %collective-permute-start.6 = (bf16[1,1,384,1536]{3,2,1,0:T(8,128)(2,1)}, bf16[1,1,384,1536]{3,2,1,0:T(8,128)(2,1)}, u32[]{:S(2)}, u32[]{:S(2)}) collective-permute-start(bf16[1,1,384,1536]{3,2,1,0:T(8,128)(2,1)} %param.16), channel_id=1, source_target_pairs={{0,12},{4,16},{8,20},{12,24},{16,28},{20,0},{24,4},{28,8},{1,13},{... | collective-permute-start | bytes 3538952 | tf_op jit(solution)/shard_map/ppermute | solution.py:34
  11.9 176.2 %collective-permute-start.5 = (bf16[1,1,384,1536]{3,2,1,0:T(8,128)(2,1)}, bf16[1,1,384,1536]{3,2,1,0:T(8,128)(2,1)}, u32[]{:S(2)}, u32[]{:S(2)}) collective-permute-start(bf16[1,1,384,1536]{3,2,1,0:T(8,128)(2,1)} %param.16), channel_id=1, source_target_pairs={{0,24},{4,28},{8,0},{12,4},{16,8},{20,12},{24,16},{28,20},{1,25},{... | collective-permute-start | bytes 3538952 | tf_op jit(solution)/shard_map/ppermute | solution.py:34
  12.1 184.5 %collective-permute-start.4 = (bf16[1,1,384,1536]{3,2,1,0:T(8,128)(2,1)}, bf16[1,1,384,1536]{3,2,1,0:T(8,128)(2,1)}, u32[]{:S(2)}, u32[]{:S(2)}) collective-permute-start(bf16[1,1,384,1536]{3,2,1,0:T(8,128)(2,1)} %param.16), channel_id=1, source_target_pairs={{0,8},{4,12},{8,16},{12,20},{16,24},{20,28},{24,0},{28,4},{1,9},{5... | collective-permute-start | bytes 3538952 | tf_op jit(solution)/shard_map/ppermute | solution.py:34
  84.9 111.7 %collective-permute-start.3 = (bf16[1,1,384,1536]{3,2,1,0:T(8,128)(2,1)}, bf16[1,1,384,1536]{3,2,1,0:T(8,128)(2,1)}, u32[]{:S(2)}, u32[]{:S(2)}) collective-permute-start(bf16[1,1,384,1536]{3,2,1,0:T(8,128)(2,1)} %param.16), channel_id=1, source_target_pairs={{0,28},{4,0},{8,4},{12,8},{16,12},{20,16},{24,20},{28,24},{1,29},{... | collective-permute-start | bytes 3538952 | tf_op jit(solution)/shard_map/ppermute | solution.py:34
  85.0 125.6 %collective-permute-start.2 = (bf16[1,1,384,1536]{3,2,1,0:T(8,128)(2,1)}, bf16[1,1,384,1536]{3,2,1,0:T(8,128)(2,1)}, u32[]{:S(2)}, u32[]{:S(2)}) collective-permute-start(bf16[1,1,384,1536]{3,2,1,0:T(8,128)(2,1)} %param.16), channel_id=1, source_target_pairs={{0,4},{4,8},{8,12},{12,16},{16,20},{20,24},{24,28},{28,0},{1,5},{5... | collective-permute-start | bytes 3538952 | tf_op jit(solution)/shard_map/ppermute | solution.py:34
  89.5 1.9 copy-start.1
  91.4 1.1 copy-start.3
  109.4 126.4 %collective-permute-start.8 = (bf16[1,1,384,1536]{3,2,1,0:T(8,128)(2,1)}, bf16[1,1,384,1536]{3,2,1,0:T(8,128)(2,1)}, u32[]{:S(2)}, u32[]{:S(2)}) collective-permute-start(bf16[1,1,384,1536]{3,2,1,0:T(8,128)(2,1)} %param.16), channel_id=1, source_target_pairs={{0,16},{4,20},{8,24},{12,28},{16,0},{20,4},{24,8},{28,12},{1,17},{... | collective-permute-start | bytes 3538952 | tf_op jit(solution)/shard_map/ppermute | solution.py:34
  188.1 49.6 %collective-permute-start.7 = (bf16[1,1,384,1536]{3,2,1,0:T(8,128)(2,1)}, bf16[1,1,384,1536]{3,2,1,0:T(8,128)(2,1)}, u32[]{:S(2)}, u32[]{:S(2)}) collective-permute-start(bf16[1,1,384,1536]{3,2,1,0:T(8,128)(2,1)} %param.16), channel_id=1, source_target_pairs={{0,20},{4,24},{8,28},{12,0},{16,4},{20,8},{24,12},{28,16},{1,21},{... | collective-permute-start | bytes 3538952 | tf_op jit(solution)/shard_map/ppermute | solution.py:34
  190.2 6.4 %copy-start.2 = (bf16[1,1,384,1536]{3,2,1,0:T(8,128)(2,1)}, bf16[1,1,384,1536]{3,2,1,0:T(8,128)(2,1)S(1)}, u32[]{:S(2)}) copy-start(bf16[1,1,384,1536]{3,2,1,0:T(8,128)(2,1)S(1)} %fusion.10) | copy-start | bytes 3538948
Sparse Core Ops, SparseCore 0:
  91.5 41.2 all-reduce.1
where the time goes:
time: 277 us; the launch traced here: 273 us
  waiting for transfers between devices  195 us (70%)
  matrix products  34.6 us (12%)
  between operations  19.2 us (7%)
  other arithmetic  12.1 us (4%)
  starting transfers between devices  8.93 us (3%)
  local copies, waits for them, and re-layouts  3.27 us (1%)
    ppermute x7, waiting for transfers between devices, passed_along(): lax.ppermute(value, axis, [(i, (i + by) % devices) for i in range(devices)])  137 us
    ppermute x1, waiting for transfers between devices, padded(): lax.ppermute(tail, axis, [(i, (i + 1) % count) for i in range(count)])  57.9 us
    dot_general x1, matrix products, local_grad(): lax.dot_general(normed, slope_bf, (((0,), (0,)), ((), ())), preferred_ele...  28.2 us
    ppermute x7, starting transfers between devices, passed_along(): lax.ppermute(value, axis, [(i, (i + by) % devices) for i in range(devices)])  7.37 us
    dot_general x1, matrix products, local_grad(): jnp.dot(normed, params, preferred_element_type=jnp.float32) * inv_root  6.41 us
  transfers between devices with their start and end apart: 10, of which 7 were waited for; matrix products, arithmetic and copies ran while one was open for 8% of the time, Pallas kernels for 0%

commit v1 on v0

--- a/solution.py
+++ b/solution.py
@@ -1,8 +1,11 @@
+import functools
 import math
 
 import jax
 import jax.numpy as jnp
 from jax import lax
+from jax.experimental import pallas as pl
+from jax.experimental.pallas import tpu as pltpu
 from jax.sharding import PartitionSpec as P
 
 ROUNDS = 4
@@ -93,7 +96,285 @@
     return (new_params, new_tracker)
 
 
+MESH = pl.DeviceIdType.MESH
+f32 = jnp.float32
+bf16 = jnp.bfloat16
+
+
+def cycle_coeffs(num_ref, den_ref, count):
+    coef = [1.0] + [0.0] * (ROUNDS + 1)
+    older = coef
+    for turn in range(ROUNDS):
+        omega = jnp.full((1, 128), num_ref[turn], jnp.int32).astype(f32) / jnp.full(
+            (1, 128), den_ref[turn], jnp.int32
+        ).astype(f32)
+        following = []
+        for dist in range(ROUNDS + 1):
+            mixed = (coef[abs(dist - 1)] + coef[dist] + coef[dist + 1]) / 3.0
+            following.append(omega * mixed + (1.0 - omega) * older[dist])
+        older, coef = (coef, following + [0.0])
+    folded = [None] * count
+    for hop in range(-ROUNDS, ROUNDS + 1):
+        at = hop % count
+        folded[at] = coef[abs(hop)] if folded[at] is None else folded[at] + coef[abs(hop)]
+    return folded
+
+
+def fused_kernel(
+    n, groups, tile,
+    num_ref, den_ref, ids_ref, hid_ref, cot_ref, win_ref, wout_ref, trk_ref, old_ref,
+    par_out, trk_out,
+    hid, cot, win, wout, trk, old,
+    wout_t, normed, normed_t, back, slope, grad,
+    rs_core, rs_send, rs_x, m_own, m_bf, m_recv, mix, params,
+    got, cons_send, cons, result,
+    load_sem, core_s, core_r, x_s, x_r, nb_s, nb_r, ag_s, ag_r, p1_s, p1_r, p2_s, p2_r,
+    po_sem, to_sem,
+):
+    b = lax.axis_index("blk")
+    g = lax.axis_index("grp")
+    rows_all, depth = hid.shape
+    width = win.shape[1]
+    part = width // groups
+    chunk = depth // n
+    core, side = lax.rem(g, 2), g // 2
+    core_peer = side * 2 + (1 - core)
+    x_peer = (1 - side) * 2 + core
+    diag = (1 - side) * 2 + (1 - core)
+    inv_root = depth ** (-0.5)
+
+    def cols(which):
+        return pl.ds(pl.multiple_of(which * part, 128), part)
+
+    def rows(which):
+        return pl.ds(pl.multiple_of(which * chunk, 16), chunk)
+
+    def ring(by):
+        return lax.rem(b + (by + n), n)
+
+    loads = [
+        pltpu.make_async_copy(s, d, load_sem.at[i])
+        for i, (s, d) in enumerate(
+            [(wout_ref, wout), (hid_ref, hid), (cot_ref, cot), (win_ref, win), (trk_ref, trk), (old_ref, old)]
+        )
+    ]
+    for load in loads:
+        load.start()
+
+    barrier = pltpu.get_barrier_semaphore()
+    for peer in (core_peer, x_peer):
+        pl.semaphore_signal(barrier, inc=1, device_id=(b, peer), device_id_type=MESH)
+    for by in range(1, n):
+        pl.semaphore_signal(barrier, inc=1, device_id=(ring(by), g), device_id_type=MESH)
+    pl.semaphore_wait(barrier, n + 1)
+
+    def remote(source, target, send, recv, to):
+        return pltpu.make_async_remote_copy(
+            src_ref=source, dst_ref=target, send_sem=send, recv_sem=recv,
+            device_id=to, device_id_type=MESH,
+        )
+
+    to_core = [
+        remote(win_ref.at[:, cols(w)], rs_core.at[i], core_s.at[i], core_r.at[i], (b, core_peer))
+        for i, w in ((1, diag), (0, core_peer))
+    ]
+    for copy in to_core:
+        copy.start()
+    first = {
+        by: remote(
+            trk_ref.at[rows(ring(by))], got.at[by], p1_s.at[by], p1_r.at[by], (ring(by), g)
+        )
+        for by in range(1, n)
+    }
+    order = sorted(range(1, n), key=lambda by: -min(by, n - by))
+    for by in order:
+        first[by].start()
+
+    loads[0].wait()
+    wout_t[...] = wout[...].T
+    loads[2].wait()
+
+    def flow(i, carry):
+        at = pl.ds(pl.multiple_of(i * tile, tile), tile)
+        back[at, :] = jnp.dot(cot[at, :], wout_t[...], preferred_element_type=f32)
+        return carry
+
+    loads[1].wait()
+
+    def norm(i, carry):
+        at = pl.ds(pl.multiple_of(i * tile, tile), tile)
+        wide = hid[at, :].astype(f32)
+        mean_square = jnp.mean(wide * wide, axis=-1, keepdims=True)
+        scaled = (wide * lax.rsqrt(mean_square + epsilon)).astype(bf16)
+        normed[at, :] = scaled
+        flipped = scaled.astype(f32).T
+        normed_t[:, at] = jnp.where(ids_ref[:, at] != 0, flipped, 0.0).astype(bf16)
+        return carry
+
+    loads[3].wait()
+    for copy in to_core:
+        copy.wait()
+    rs_send[...] = (win[:, cols(x_peer)].astype(f32) + rs_core[1].astype(f32)).astype(bf16)
+    to_x = remote(rs_send, rs_x, x_s.at[0], x_r.at[0], (b, x_peer))
+    to_x.start()
+    m_own[...] = win[:, cols(g)].astype(f32) + rs_core[0].astype(f32)
+    lax.fori_loop(0, rows_all // tile, norm, 0)
+    to_x.wait()
+    m_own[...] += rs_x[...].astype(f32)
+    m_bf[...] = m_own[...].astype(bf16)
+    beside = [
+        remote(m_bf, m_recv.at[i], nb_s.at[i], nb_r.at[i], (ring(by), g))
+        for i, by in ((0, 1), (1, -1))
+    ]
+    for copy in beside:
+        copy.start()
+    lax.fori_loop(0, rows_all // tile, flow, 0)
+
+    loads[4].wait()
+    loads[5].wait()
+    for by in order:
+        first[by].wait()
+    got[0] = trk[rows(b), :]
+    coef = cycle_coeffs(num_ref, den_ref, n)
+    lanes = coef[0].shape[1]
+
+    def combine(i, carry):
+        at = pl.ds(pl.multiple_of(i * lanes, lanes), lanes)
+        parts = [got[by, :, at].astype(f32) for by in range(n)]
+        for to in range(n):
+            total = coef[to] * parts[0]
+            for by in range(1, n):
+                total = total + coef[(to + by) % n] * parts[by]
+            if to == 0:
+                cons[rows(b), at] = total.astype(bf16)
+            else:
+                cons_send[to, :, at] = total.astype(bf16)
+        return carry
+
+    lax.fori_loop(0, width // lanes, combine, 0)
+    second = {
+        by: remote(cons_send.at[by], cons.at[rows(b)], p2_s.at[by], p2_r.at[by], (ring(by), g))
+        for by in range(1, n)
+    }
+    for by in order:
+        second[by].start()
+
+    for copy in beside:
+        copy.wait()
+    mix[0] = (
+        (m_own[...] + m_recv[0].astype(f32) + m_recv[1].astype(f32)) / (3.0 * groups)
+    ).astype(bf16)
+    gather = [
+        remote(mix.at[0], mix.at[1], ag_s.at[0], ag_r.at[0], (b, x_peer)),
+        remote(mix.at[0], mix.at[2], ag_s.at[1], ag_r.at[1], (b, core_peer)),
+        remote(mix.at[1], mix.at[3], ag_s.at[2], ag_r.at[2], (b, core_peer)),
+    ]
+    gather[0].start()
+    gather[1].start()
+
+    written = []
+    for slot, owner in ((0, g), (2, core_peer), (1, x_peer), (3, diag)):
+        if slot == 2:
+            gather[1].wait()
+        if slot == 1:
+            gather[0].wait()
+            gather[2].start()
+        if slot == 3:
+            gather[2].wait()
+        here = cols(owner)
+        params[slot] = (
+            mix[slot].astype(f32) - step_size * trk[:, here].astype(f32)
+        ).astype(bf16)
+        copy = pltpu.make_async_copy(params.at[slot], par_out.at[:, here], po_sem.at[slot])
+        copy.start()
+        written.append(copy)
+
+        def tokens(i, carry, slot=slot, here=here):
+            at = pl.ds(pl.multiple_of(i * tile, tile), tile)
+            p = jnp.dot(normed[at, :], params[slot], preferred_element_type=f32) * inv_root
+            square = p * p
+            bent = jnp.tanh(p * (tanh_scale + (tanh_scale * 0.044715) * square))
+            ramp = p * (tanh_scale + (3.0 * 0.044715 * tanh_scale) * square)
+            bend = (1.0 + bent) * (1.0 + (1.0 - bent) * ramp)
+            slope[at, :] = (back[at, here] * (0.5 * bend)).astype(bf16)
+            return carry
+
+        lax.fori_loop(0, rows_all // tile, tokens, 0)
+        grad[:, here] = (
+            jnp.dot(normed_t[...], slope[...], preferred_element_type=f32) * inv_root
+            - old[:, here].astype(f32)
+        )
+
+    for by in [0] + order:
+        if by:
+            second[by].wait()
+        here = rows(ring(-by))
+        result[here, :] = (grad[here, :] + cons[here, :].astype(f32)).astype(bf16)
+        copy = pltpu.make_async_copy(result.at[here], trk_out.at[here], to_sem.at[by])
+        copy.start()
+        written.append(copy)
+    for copy in written:
+        copy.wait()
+
+
+def fused_shards(hidden, cotangent, token_ids, w_in, w_out, tracker, grad_old, cheb_num, cheb_den):
+    n, groups = lax.axis_size("blk"), lax.axis_size("grp")
+    tokens, depth = hidden.shape
+    width = w_in.shape[-1]
+    part, chunk = width // groups, depth // n
+    tile = 256
+    leaf = jax.ShapeDtypeStruct((depth, width), bf16)
+    hbm, smem, vmem = (
+        pl.BlockSpec(memory_space=space) for space in (pl.ANY, pltpu.SMEM, pltpu.VMEM)
+    )
+    dma = pltpu.SemaphoreType.DMA
+    new_params, new_tracker = pl.pallas_call(
+        functools.partial(fused_kernel, n, groups, tile),
+        out_shape=(leaf, leaf),
+        in_specs=[smem, smem, vmem] + [hbm] * 6,
+        out_specs=(hbm, hbm),
+        scratch_shapes=[
+            pltpu.VMEM((tokens, depth), bf16),
+            pltpu.VMEM((tokens, depth), bf16),
+            pltpu.VMEM((depth, width), bf16),
+            pltpu.VMEM((width, depth), bf16),
+            pltpu.VMEM((depth, width), bf16),
+            pltpu.VMEM((depth, width), bf16),
+            pltpu.VMEM((depth, width), bf16),
+            pltpu.VMEM((tokens, depth), bf16),
+            pltpu.VMEM((depth, tokens), bf16),
+            pltpu.VMEM((tokens, width), f32),
+            pltpu.VMEM((tokens, part), bf16),
+            pltpu.VMEM((depth, width), f32),
+            pltpu.VMEM((2, depth, part), bf16),
+            pltpu.VMEM((depth, part), bf16),
+            pltpu.VMEM((depth, part), bf16),
+            pltpu.VMEM((depth, part), f32),
+            pltpu.VMEM((depth, part), bf16),
+            pltpu.VMEM((2, depth, part), bf16),
+            pltpu.VMEM((4, depth, part), bf16),
+            pltpu.VMEM((4, depth, part), bf16),
+            pltpu.VMEM((n, chunk, width), bf16),
+            pltpu.VMEM((n, chunk, width), bf16),
+            pltpu.VMEM((depth, width), bf16),
+            pltpu.VMEM((depth, width), bf16),
+            dma((6,)), dma((2,)), dma((2,)), dma((1,)), dma((1,)), dma((2,)), dma((2,)),
+            dma((3,)), dma((3,)), dma((n,)), dma((n,)), dma((n,)), dma((n,)),
+            dma((4,)), dma((n,)),
+        ],
+        compiler_params=pltpu.CompilerParams(
+            collective_id=0, has_side_effects=True, vmem_limit_bytes=60 * 2**20
+        ),
+    )(
+        cheb_num, cheb_den, token_ids.reshape(1, tokens), hidden, cotangent,
+        w_in[0, 0], w_out, tracker[0, 0], grad_old[0, 0],
+    )
+    return new_params[None, None], new_tracker[None, None]
+
+
 def solution(mesh):
+    n, groups = mesh.shape["blk"], mesh.shape["grp"]
+    fused = 2 < n <= 2 * ROUNDS and groups == 4
     placed = (
         P(("blk", "grp"), None),
         P(("blk", "grp"), None),
@@ -106,7 +387,7 @@
         P(),
     )
     return jax.shard_map(
-        shards,
+        fused_shards if fused else shards,
         mesh=mesh,
         in_specs=placed,
         out_specs=(P("blk", "grp", None, None), P("blk", "grp", None, None)),

time: 277 us -> 75.3 us (0.27); the launches traced: 273 us -> 74.6 us
  waiting for transfers between devices: 195 us -> 0 us
  Pallas kernels: 0 us -> 70.5 us
  matrix products: 34.6 us -> 0 us
  between operations: 19.2 us -> 0.65 us
  other arithmetic: 12.1 us -> 0 us
  starting transfers between devices: 8.93 us -> 0 us
    ppermute x9 -> x0, waiting for transfers between devices: 195 us -> none  [the longest x7 137 us: passed_along(): lax.ppermute(value, axis, [(i, (i + by) % devices) for i in range(devices)])]
    pallas_call x0 -> x1, Pallas kernels: none -> 70.5 us  [fused_shards(): pl.pallas_call(functools.partial(fused_kernel, n, groups, tile), out_shap...]
    dot_general x2 -> x0, matrix products: 34.6 us -> none  [the longest x1 28.2 us: local_grad(): lax.dot_general(normed, slope_bf, (((0,), (0,)), ((), ())), preferred_ele...]
    ppermute x9 -> x0, starting transfers between devices: 8.89 us -> none  [the longest x7 7.37 us: passed_along(): lax.ppermute(value, axis, [(i, (i + by) % devices) for i in range(devices)])]
    convert_element_type x3 -> x0, other arithmetic: 5.71 us -> none  [the longest x1 2.05 us: shards(): (group_avg - step_size * tracker.astype(jnp.float32)).astype(jnp.bfloat16)]
    add x4 -> x0, other arithmetic: 5.34 us -> none  [shards(): weights[turn_idx] * mixed_coef + (1.0 - weights[turn_idx]) * older_coef]
    unnamed x8 -> x4, local copies, waits for them, and re-layouts: 0.03 us -> 3.47 us
    slice x8 -> x0, local copies, waits for them, and re-layouts: 3.24 us -> none  [the longest x6 1.97 us: shards(): jnp.roll(current_coef, 1) + current_coef + jnp.roll(current_coef, -1)]
  transfers between devices with their start and end apart: 10 -> 0, of which waited for: 7 -> 0; matrix products, arithmetic and copies ran while one was open for 8% -> 0% of each run, Pallas kernels for 0% -> 0%
where the time goes in v1:
time: 75.3 us; the launch traced here: 74.6 us
  Pallas kernels  70.5 us (94%)
  local copies, waits for them, and re-layouts  3.47 us (5%)
    pallas_call x1, Pallas kernels, fused_shards(): pl.pallas_call(functools.partial(fused_kernel, n, groups, tile), out_shap...  70.5 us
    unnamed x4, local copies, waits for them, and re-layouts  3.47 us

profile of v1, /device:TPU:13, one launch (start us, length us, event | category | flops | bytes accessed | tf_op | source)
XLA Modules:
  0.0 74.6 jit_solution(6539463387769200302)
XLA Ops:
  0.6 70.5 %shard_map.104 = (bf16[384,1536]{1,0:T(8,128)(2,1)}, bf16[384,1536]{1,0:T(8,128)(2,1)}) custom-call(s32[4]{0:T(128)} %num_ref.1, s32[4]{0:T(128)} %den_ref.1, s32[1,2048]{1,0:T(1,128)} %bitcast.11, bf16[2048,384]{1,0:T(8,128)(2,1)} %hid_ref.1, bf16[2048,384]{1,0:T(8,128)(2,1)} %cot_ref.1, bf16[384,1536]{1,0:T(8,128)(2,1)} %bitcast.6, ...), custom_call_target="tpu_custom_call" | custom-call | tf_op jit(solution)/shard_map/pallas_call | solution.py:331
  71.1 0.0 copy-start
  71.1 2.5 %copy.13 = bf16[1,1,384,1536]{3,2,1,0:T(8,128)(2,1)} copy(bf16[1,1,384,1536]{3,2,1,0:T(8,128)(2,1)} %bitcast.10) | data formatting | bytes 2359296
  73.6 0.0 copy-done
  73.6 1.0 %copy.14 = bf16[1,1,384,1536]{3,2,1,0:T(8,128)(2,1)} copy(bf16[1,1,384,1536]{3,2,1,0:T(8,128)(2,1)S(1)} %bitcast.9) | data formatting | bytes 2359296
Async XLA Ops:
  71.1 2.5 %copy-start = (bf16[384,1536]{1,0:T(8,128)(2,1)S(1)}, bf16[384,1536]{1,0:T(8,128)(2,1)}, u32[]{:S(2)}) copy-start(bf16[384,1536]{1,0:T(8,128)(2,1)} %get-tuple-element.5) | copy-start | bytes 3538948

commit v2 on v1

--- a/solution.py
+++ b/solution.py
@@ -187,7 +187,7 @@
         for by in range(1, n)
     }
     order = sorted(range(1, n), key=lambda by: -min(by, n - by))
-    for by in order:
+    for by in order[:3]:
         first[by].start()
 
     loads[0].wait()
@@ -228,7 +228,8 @@
     ]
     for copy in beside:
         copy.start()
-    lax.fori_loop(0, rows_all // tile, flow, 0)
+    for by in order[3:]:
+        first[by].start()
 
     loads[4].wait()
     loads[5].wait()
@@ -258,6 +259,7 @@
     }
     for by in order:
         second[by].start()
+    lax.fori_loop(0, rows_all // tile, flow, 0)
 
     for copy in beside:
         copy.wait()

time: 75.3 us -> 72.6 us (0.964)
  Pallas kernels: 70.5 us -> 68.3 us
    pallas_call x1, Pallas kernels: 70.5 us -> 68.3 us  [fused_shards(): pl.pallas_call(functools.partial(fused_kernel, n, groups, tile), out_shap...]
where the time goes in v2:
time: 72.6 us; the launch traced here: 72.4 us
  Pallas kernels  68.3 us (94%)
  local copies, waits for them, and re-layouts  3.47 us (5%)
    pallas_call x1, Pallas kernels, fused_shards(): pl.pallas_call(functools.partial(fused_kernel, n, groups, tile), out_shap...  68.3 us
    unnamed x4, local copies, waits for them, and re-layouts  3.47 us

profile of v2, /device:TPU:13, one launch (start us, length us, event | category | flops | bytes accessed | tf_op | source)
XLA Modules:
  0.0 72.4 jit_solution(107525122407978125)
XLA Ops:
  0.6 68.3 %shard_map.104 = (bf16[384,1536]{1,0:T(8,128)(2,1)}, bf16[384,1536]{1,0:T(8,128)(2,1)}) custom-call(s32[4]{0:T(128)} %num_ref.1, s32[4]{0:T(128)} %den_ref.1, s32[1,2048]{1,0:T(1,128)} %bitcast.11, bf16[2048,384]{1,0:T(8,128)(2,1)} %hid_ref.1, bf16[2048,384]{1,0:T(8,128)(2,1)} %cot_ref.1, bf16[384,1536]{1,0:T(8,128)(2,1)} %bitcast.6, ...), custom_call_target="tpu_custom_call" | custom-call | tf_op jit(solution)/shard_map/pallas_call | solution.py:333
  68.9 0.0 copy-start
  69.0 2.5 %copy.13 = bf16[1,1,384,1536]{3,2,1,0:T(8,128)(2,1)} copy(bf16[1,1,384,1536]{3,2,1,0:T(8,128)(2,1)} %bitcast.10) | data formatting | bytes 2359296
  71.4 0.0 copy-done
  71.4 1.0 %copy.14 = bf16[1,1,384,1536]{3,2,1,0:T(8,128)(2,1)} copy(bf16[1,1,384,1536]{3,2,1,0:T(8,128)(2,1)S(1)} %bitcast.9) | data formatting | bytes 2359296
Async XLA Ops:
  68.9 2.5 %copy-start = (bf16[384,1536]{1,0:T(8,128)(2,1)S(1)}, bf16[384,1536]{1,0:T(8,128)(2,1)}, u32[]{:S(2)}) copy-start(bf16[384,1536]{1,0:T(8,128)(2,1)} %get-tuple-element.5) | copy-start | bytes 3538948

commit v3 on v2

--- a/solution.py
+++ b/solution.py
@@ -324,7 +324,7 @@
     tokens, depth = hidden.shape
     width = w_in.shape[-1]
     part, chunk = width // groups, depth // n
-    tile = 256
+    tile = 512
     leaf = jax.ShapeDtypeStruct((depth, width), bf16)
     hbm, smem, vmem = (
         pl.BlockSpec(memory_space=space) for space in (pl.ANY, pltpu.SMEM, pltpu.VMEM)

time: 72.6 us -> 72.6 us (level)
  no operation moved by 1% of the time
where the time goes in v3:
time: 72.6 us; the launch traced here: 72.4 us
  Pallas kernels  68.3 us (94%)
  local copies, waits for them, and re-layouts  3.47 us (5%)
    pallas_call x1, Pallas kernels, fused_shards(): pl.pallas_call(functools.partial(fused_kernel, n, groups, tile), out_shap...  68.3 us
    unnamed x4, local copies, waits for them, and re-layouts  3.47 us

profile of v3, /device:TPU:13, one launch (start us, length us, event | category | flops | bytes accessed | tf_op | source)
XLA Modules:
  0.0 72.4 jit_solution(17935762152962725428)
XLA Ops:
  0.6 68.3 %shard_map.104 = (bf16[384,1536]{1,0:T(8,128)(2,1)}, bf16[384,1536]{1,0:T(8,128)(2,1)}) custom-call(s32[4]{0:T(128)} %num_ref.1, s32[4]{0:T(128)} %den_ref.1, s32[1,2048]{1,0:T(1,128)} %bitcast.11, bf16[2048,384]{1,0:T(8,128)(2,1)} %hid_ref.1, bf16[2048,384]{1,0:T(8,128)(2,1)} %cot_ref.1, bf16[384,1536]{1,0:T(8,128)(2,1)} %bitcast.6, ...), custom_call_target="tpu_custom_call" | custom-call | tf_op jit(solution)/shard_map/pallas_call | solution.py:333
  68.9 0.0 copy-start
  69.0 2.5 %copy.13 = bf16[1,1,384,1536]{3,2,1,0:T(8,128)(2,1)} copy(bf16[1,1,384,1536]{3,2,1,0:T(8,128)(2,1)} %bitcast.10) | data formatting | bytes 2359296
  71.4 0.0 copy-done
  71.4 1.0 %copy.14 = bf16[1,1,384,1536]{3,2,1,0:T(8,128)(2,1)} copy(bf16[1,1,384,1536]{3,2,1,0:T(8,128)(2,1)S(1)} %bitcast.9) | data formatting | bytes 2359296
Async XLA Ops:
  68.9 2.5 %copy-start = (bf16[384,1536]{1,0:T(8,128)(2,1)S(1)}, bf16[384,1536]{1,0:T(8,128)(2,1)}, u32[]{:S(2)}) copy-start(bf16[384,1536]{1,0:T(8,128)(2,1)} %get-tuple-element.5) | copy-start | bytes 3538948
